TPU v7x, 256 devices: a whole 4x4x8 slice. The times are simulated.
256 devices in a mesh: feeder: 64 (over z, x, core), node: 4 (over y).
Axes of the slice: x: 4, y: 4, z: 8, core: 2. Of those that a mesh axis runs over, the one named last changes fastest.
Arguments:
- factors: bfloat16 [2048, 256], P('node'), may hold values from -6 to 6
- loadings: bfloat16 [32768, 256], P(('feeder', 'node')), may hold values from -0.35355339 to 0.5
- parents: int32 [32768], P(('feeder', 'node')), may hold values from -1 to 126, as said below
- load_base: float32 [2, 32768], P(None, ('feeder', 'node')), may hold values from 2.4414063e-06 to 0.00048828125, as said below
- lateral_z: float32 [2, 32768], P(None, ('feeder', 'node')), may hold values from 0.007 to 0.175, as said below
- trunk_z: float32 [2, 64, 4], P(None, 'feeder', 'node'), may hold values from 0.00034375 to 0.00609375, as said below
Outputs:
- volt_real: float32 [2048, 32768], P(None, ('feeder', 'node'))
- volt_imag: float32 [2048, 32768], P(None, ('feeder', 'node'))
Inputs may be any that keep to these rules, and one draw needn't show every extreme that they name: `parents`: within each aligned run of 128 nodes (one lateral), a node's entry is the position of its parent in the same lateral, which comes before it, or -1 for a branch from the section's head node; the first node of every lateral has -1 and the last node's parent is the node just before it. `load_base`: with unit = 1 / 8192, row 0 lies between 1 and 4 units and row 1 between 0.02 and 0.08 units. `lateral_z`: with unit = 128 * 64 / 128^2, row 0 lies between 0.014 and 0.056 units and row 1 between 0.087 and 0.35 units. `trunk_z`: with unit = 1 / 64, row 0 lies between 0.022 and 0.066 units and row 1 between 0.13 and 0.39 units.
All inputs are finite; a program needn't handle non-finite values.
Results may differ from a plain program's by a relative error of at most 0.0003.
Values may be sent and summed in bfloat16 or wider, within the bound.
A program may use at most 64 MiB of HBM per device.

v0:
```python
import jax
import jax.numpy as jnp
from jax import lax
from jax.sharding import PartitionSpec as P

LAT_NODES = 128
SWEEPS = 3
HIGHEST = lax.Precision.HIGHEST


def carried_in(part, axis, combine, identity, reverse):
    count = lax.axis_size(axis)
    place = lax.axis_index(axis)
    ahead = count - 1 - place if reverse else place
    gathered = lax.all_gather(part, axis)
    state = jnp.zeros_like(part) + jnp.asarray(identity, part.dtype)

    def one(turn, state):
        source = count - 1 - turn if reverse else turn
        return combine(state, lax.dynamic_index_in_dim(gathered, source, 0, False))

    return lax.fori_loop(0, ahead, one, state)


def path_matrix(parent_rows):
    laterals, width = parent_rows.shape
    column = jnp.arange(width, dtype=jnp.int32)
    adjacency = (parent_rows[:, :, None] == column[None, None, :]).astype(jnp.float32)
    identity = jnp.eye(width, dtype=jnp.float32)
    paths = identity[None] + adjacency
    power = adjacency
    for turn in range((width - 1).bit_length() - 1):
        power = jnp.einsum("alm,amn->aln", power, power, precision=HIGHEST)
        paths = paths + jnp.einsum("alm,amn->aln", paths, power, precision=HIGHEST)
    return paths


def node_currents(active, reactive, real_part, imag_part):
    magnitude = real_part * real_part + imag_part * imag_part
    return (
        (active * real_part + reactive * imag_part) / magnitude,
        (active * imag_part - reactive * real_part) / magnitude,
    )


def add_total(earlier, later):
    return earlier + later


def lateral_products(stacked, tables):
    blocks = jnp.dot(stacked, tables[0], precision=HIGHEST, preferred_element_type=jnp.float32)
    return blocks


def trunk_heads(inject, trunk_z, scen):
    resist_trunk = trunk_z[0, 0, 0]
    react_trunk = trunk_z[1, 0, 0]
    zeros = jnp.zeros_like(inject)
    beyond = carried_in(inject, "feeder", add_total, zeros, True)
    trunk = inject + beyond
    trunk_real = trunk[:scen]
    trunk_imag = trunk[scen:]
    drop = jnp.concatenate(
        [
            resist_trunk * trunk_real - react_trunk * trunk_imag,
            resist_trunk * trunk_imag + react_trunk * trunk_real,
        ]
    )
    before = carried_in(drop, "feeder", add_total, zeros, False)
    total = before + drop
    return (1.0 - total[:scen], -total[scen:])


def local(factors, loadings, parents, load_base, lateral_z, trunk_z):
    levels = jnp.einsum(
        "sr,nr->sn",
        lax.all_gather(factors, "node", axis=0, tiled=True),
        loadings,
        preferred_element_type=jnp.float32,
    ).astype(jnp.bfloat16)
    scen = levels.shape[0]
    nodes_here = levels.shape[1]
    lat_count = nodes_here // LAT_NODES
    swing = 1.0 + 0.5 * jnp.tanh(levels.astype(jnp.float32))
    active = load_base[0][None, :] * swing
    reactive = load_base[1][None, :] * swing
    paths = path_matrix(parents.reshape(lat_count, LAT_NODES))
    paths_back = jnp.swapaxes(paths, 1, 2)
    resist = lateral_z[0][None, :]
    react = lateral_z[1][None, :]
    volts = jnp.concatenate(
        [jnp.ones((scen, nodes_here), jnp.float32), jnp.zeros((scen, nodes_here), jnp.float32)]
    )
    for sweep_index in range(SWEEPS):
        current_real, current_imag = node_currents(active, reactive, volts[:scen], volts[scen:])
        current = jnp.concatenate([current_real, current_imag])
        inject = jnp.sum(current, axis=1)
        branch = lateral_products(current, paths)
        branch_real = branch[:scen]
        branch_imag = branch[scen:]
        weighted = jnp.concatenate(
            [resist * branch_real - react * branch_imag, resist * branch_imag + react * branch_real]
        )
        drops = lateral_products(weighted, paths_back)
        head_real, head_imag = trunk_heads(inject, trunk_z, scen)
        volts = jnp.concatenate(
            [head_real[:, None] - drops[:scen], head_imag[:, None] - drops[scen:]]
        )
    return (volts[:scen], volts[scen:])


def solution(mesh):
    return jax.shard_map(
        local,
        mesh=mesh,
        in_specs=(
            P("node", None),
            P(("feeder", "node"), None),
            P(("feeder", "node")),
            P(None, ("feeder", "node")),
            P(None, ("feeder", "node")),
            P(None, "feeder", "node"),
        ),
        out_specs=(P(None, ("feeder", "node")), P(None, ("feeder", "node"))),
        check_vma=False,
    )
```

profile of v0, /device:TPU:1, one launch (start us, length us, event | category | flops | bytes accessed | tf_op | source)
XLA Modules:
  0.0 646.7 jit_solution(12022927235953794426)
XLA Ops:
  8.7 29.5 %all-gather.14.cloned.1.call-done = bf16[2048,256]{1,0:T(8,128)(2,1)} async-done(((bf16[512,256]{1,0:T(8,128)(2,1)}), bf16[2048,256]{1,0:T(8,128)(2,1)}) %all-gather.14.cloned.1.call-update) | async-done | bytes 1048592 | tf_op jit(solution)/shard_map/all_gather | solution.py:77
  38.2 1.7 multiply_add_fusion.5
  40.0 1.2 fusion.21
  43.6 77.6 %all-gather.16.cloned.1.call-done = f32[262144]{0:T(1024)} async-done(((f32[4096]{0:T(1024)}), f32[262144]{0:T(1024)}) %all-gather.16.cloned.1.call-update) | async-done | bytes 1048592 | tf_op jit(solution)/shard_map/all_gather | solution.py:15
  121.2 2.4 reshape.172
  123.6 59.7 %while.66 = (s32[]{:T(128)}, f32[4096]{0:T(1024)S(1)}, s32[]{:T(128)}, f32[64,4096]{1,0:T(8,128)}, s32[]{:T(128)}, /*index=5*/s32[]{:T(128)}, s32[]{:T(128)}, s32[]{:T(128)}) while((s32[]{:T(128)}, f32[4096]{0:T(1024)S(1)}, s32[]{:T(128)}, f32[64,4096]{1,0:T(8,128)}, s32[]{:T(128)}, /*index=5*/s32[]{:T(128)}, s32[]{:T(128)}, s32[]{:T(128)}) %tuple.128), condition=%wide.region_2.3_spmd, body=%wide.region_1.2_spmd.sunk | while | flops 4102 | bytes 82055 | solution.py:22
  183.3 1.2 multiply_subtract_fusion.6
  186.0 1.9 fusion.20
  188.2 3.2 fusion.4
  191.3 65.4 %all-gather.18.cloned.1.call-done = f32[262144]{0:T(1024)} async-done(((f32[4096]{0:T(1024)}), f32[262144]{0:T(1024)}) %all-gather.18.cloned.1.call-update) | async-done | bytes 1048592 | tf_op jit(solution)/shard_map/all_gather | solution.py:15
  256.7 1.4 reshape.173
  258.2 2.0 fusion.23
  260.2 1.2 fusion.19
  261.5 77.3 %all-gather.20.cloned.1.call-done = f32[262144]{0:T(1024)} async-done(((f32[4096]{0:T(1024)}), f32[262144]{0:T(1024)}) %all-gather.20.cloned.1.call-update) | async-done | bytes 1048592 | tf_op jit(solution)/shard_map/all_gather | solution.py:15
  338.8 2.4 reshape.174
  341.2 59.7 %while.68 = (s32[]{:T(128)}, f32[4096]{0:T(1024)S(1)}, s32[]{:T(128)}, f32[64,4096]{1,0:T(8,128)}, s32[]{:T(128)}, /*index=5*/s32[]{:T(128)}, s32[]{:T(128)}, s32[]{:T(128)}) while((s32[]{:T(128)}, f32[4096]{0:T(1024)S(1)}, s32[]{:T(128)}, f32[64,4096]{1,0:T(8,128)}, s32[]{:T(128)}, /*index=5*/s32[]{:T(128)}, s32[]{:T(128)}, s32[]{:T(128)}) %tuple.134), condition=%wide.region_7.8_spmd, body=%wide.region_6.7_spmd.sunk | while | flops 4102 | bytes 82055 | solution.py:22
  400.9 1.2 multiply_subtract_fusion.5
  403.0 1.9 fusion.18
  405.1 3.2 fusion.8
  408.3 66.1 %all-gather.22.cloned.1.call-done = f32[262144]{0:T(1024)} async-done(((f32[4096]{0:T(1024)}), f32[262144]{0:T(1024)}) %all-gather.22.cloned.1.call-update) | async-done | bytes 1048592 | tf_op jit(solution)/shard_map/all_gather | solution.py:15
  474.3 1.4 reshape.175
  475.9 2.0 fusion.22
  477.9 1.2 fusion.17
  479.2 77.3 %all-gather.24.cloned.1.call-done = f32[262144]{0:T(1024)} async-done(((f32[4096]{0:T(1024)}), f32[262144]{0:T(1024)}) %all-gather.24.cloned.1.call-update) | async-done | bytes 1048592 | tf_op jit(solution)/shard_map/all_gather | solution.py:15
  556.5 1.4 reshape.176
  557.9 4.0 while.70
  562.0 1.2 multiply_subtract_fusion.4
  563.8 1.9 fusion.16
  565.9 1.8 fusion.12
  567.7 68.9 %all-gather.26.cloned.1.call-done = f32[262144]{0:T(1024)} async-done(((f32[4096]{0:T(1024)}), f32[262144]{0:T(1024)}) %all-gather.26.cloned.1.call-update) | async-done | bytes 1048592 | tf_op jit(solution)/shard_map/all_gather | solution.py:15
  636.6 1.4 reshape.177
  638.2 1.7 slice_subtract_fusion
  (445 shorter events, 124.6 us)
Async XLA Ops:
  7.2 31.1 %copy-start = (bf16[128,256]{1,0:T(8,128)(2,1)S(1)}, bf16[128,256]{1,0:T(8,128)(2,1)}, u32[]{:S(2)}) copy-start(bf16[128,256]{1,0:T(8,128)(2,1)} %param.19) | copy-start | bytes 196612
  7.2 31.0 %all-gather.14.cloned.1.call-start = ((), (), s32[]{:S(2)}) async-start(), calls=%async_computation | async-start | bytes 1310720 | tf_op jit(solution)/shard_map/all_gather | solution.py:77
  7.9 113.3 %all-gather.16.cloned.1.call-start = ((), (), s32[]{:S(2)}) async-start(), calls=%async_computation.1 | async-start | bytes 1064960 | tf_op jit(solution)/shard_map/all_gather | solution.py:15
  40.0 1.3 copy-start.5
  40.0 1.9 copy-start.4
  41.2 142.0 %copy-start.1 = (f32[4096]{0:T(1024)S(1)}, f32[4096]{0:T(1024)}, u32[]{:S(2)}) copy-start(f32[4096]{0:T(1024)} %fusion.21) | copy-start | bytes 49156
  41.2 215.4 %all-gather.18.cloned.1.call-start = ((), (), s32[]{:S(2)}) async-start(), calls=%async_computation.2 | async-start | bytes 1064960 | tf_op jit(solution)/shard_map/all_gather | solution.py:15
  42.1 143.1 %copy-start.6 = (f32[2,128]{1,0:T(2,128)S(1)}, f32[2,128]{1,0:T(2,128)}, u32[]{:S(2)}) copy-start(f32[2,128]{1,0:T(2,128)} %param.22) | copy-start | bytes 3076
  185.1 153.7 %all-gather.20.cloned.1.call-start = ((), (), s32[]{:S(2)}) async-start(), calls=%async_computation.3 | async-start | bytes 1064960 | tf_op jit(solution)/shard_map/all_gather | solution.py:15
  261.4 139.5 %copy-start.3 = (f32[4096]{0:T(1024)S(1)}, f32[4096]{0:T(1024)}, u32[]{:S(2)}) copy-start(f32[4096]{0:T(1024)} %fusion.19) | copy-start | bytes 49156
  261.4 212.9 %all-gather.22.cloned.1.call-start = ((), (), s32[]{:S(2)}) async-start(), calls=%async_computation.4 | async-start | bytes 1064960 | tf_op jit(solution)/shard_map/all_gather | solution.py:15
  402.8 153.7 %all-gather.24.cloned.1.call-start = ((), (), s32[]{:S(2)}) async-start(), calls=%async_computation.5 | async-start | bytes 1064960 | tf_op jit(solution)/shard_map/all_gather | solution.py:15
  479.1 82.9 %copy-start.2 = (f32[4096]{0:T(1024)S(1)}, f32[4096]{0:T(1024)}, u32[]{:S(2)}) copy-start(f32[4096]{0:T(1024)} %fusion.17) | copy-start | bytes 49156
  479.1 157.5 %all-gather.26.cloned.1.call-start = ((), (), s32[]{:S(2)}) async-start(), calls=%async_computation.6 | async-start | bytes 1064960 | tf_op jit(solution)/shard_map/all_gather | solution.py:15
Sparse Core Ops, SparseCore 0:
  9.8 28.3 all-gather.13
  41.6 79.5 all-gather.15
  185.2 71.4 all-gather.17
  261.6 77.2 all-gather.19
  402.9 71.4 all-gather.21
  479.2 77.2 all-gather.23
  563.9 72.6 all-gather.25
where the time goes:
time: 649 us; the launch traced here: 647 us
  waiting for transfers between devices  463 us (71%)
  local copies, waits for them, and re-layouts  127 us (20%)
  matrix products  18 us (3%)
  other arithmetic  16.4 us (3%)
  between operations  14.6 us (2%)
  loops' own time  6.86 us (1%)
    all_gather x6, waiting for transfers between devices, carried_in(): gathered = lax.all_gather(part, axis)  433 us
    dynamic_slice x189, local copies, waits for them, and re-layouts, one(): return combine(state, lax.dynamic_index_in_dim(gathered, source, 0, False))  116 us
    all_gather x1, waiting for transfers between devices, local(): lax.all_gather(factors, 'node', axis=0, tiled=True)  29.5 us
    dot_general x6, matrix products, lateral_products(): jnp.dot(stacked, tables[0], precision=HIGHEST, preferred_element_type=jnp...  13.8 us
  transfers between devices with their start and end apart: 7, of which 7 were waited for; matrix products, arithmetic and copies ran while one was open for 3% of the time, Pallas kernels for 0%

commit v1 on v0

--- a/solution.py
+++ b/solution.py
@@ -6,6 +6,11 @@
 LAT_NODES = 128
 SWEEPS = 3
 HIGHEST = lax.Precision.HIGHEST
+
+
+def exchange_gather(x, name, d):
+    stack = jnp.stack([x] * lax.axis_size(name))
+    return jnp.concatenate(lax.all_to_all(stack, name, 0, 0), axis=d)
 
 
 def carried_in(part, axis, combine, identity, reverse):
@@ -74,7 +79,7 @@
 def local(factors, loadings, parents, load_base, lateral_z, trunk_z):
     levels = jnp.einsum(
         "sr,nr->sn",
-        lax.all_gather(factors, "node", axis=0, tiled=True),
+        exchange_gather(factors, "node", 0),
         loadings,
         preferred_element_type=jnp.float32,
     ).astype(jnp.bfloat16)

time: 649 us -> 697 us (1.074)
  local copies, waits for them, and re-layouts: 127 us -> 187 us
  waiting for transfers between devices: 463 us -> 445 us
    dynamic_slice x189, local copies, waits for them, and re-layouts: 116 us -> 172 us  [one(): return combine(state, lax.dynamic_index_in_dim(gathered, source, 0, False))]
    all_gather x1 -> x0, waiting for transfers between devices: 29.5 us -> none  [local(): lax.all_gather(factors, 'node', axis=0, tiled=True)]
    all_to_all x0 -> x1, waiting for transfers between devices: none -> 13.5 us  [exchange_gather(): return jnp.concatenate(lax.all_to_all(stack, name, 0, 0), axis=d)]
where the time goes in v1:
time: 697 us; the launch traced here: 693 us
  waiting for transfers between devices  445 us (64%)
  local copies, waits for them, and re-layouts  187 us (27%)
  matrix products  18.1 us (3%)
  other arithmetic  16.4 us (2%)
  between operations  14.5 us (2%)
    all_gather x6, waiting for transfers between devices, carried_in(): gathered = lax.all_gather(part, axis)  432 us
    dynamic_slice x189, local copies, waits for them, and re-layouts, one(): return combine(state, lax.dynamic_index_in_dim(gathered, source, 0, False))  172 us
  transfers between devices with their start and end apart: 7, of which 7 were waited for; matrix products, arithmetic and copies ran while one was open for 3% of the time, Pallas kernels for 0%

profile of v1, /device:TPU:1, one launch (start us, length us, event | category | flops | bytes accessed | tf_op | source)
XLA Modules:
  0.0 692.8 jit_solution(8504464732582287394)
XLA Ops:
  7.2 2.0 stack.2
  9.2 5.0 all-to-all-start
  14.2 13.5 %all-to-all-done = bf16[4,512,256]{2,1,0:T(8,128)(2,1)S(1)} async-done(((bf16[4,512,256]{2,1,0:T(8,128)(2,1)}), bf16[4,512,256]{2,1,0:T(8,128)(2,1)S(1)}, u32[]{:S(2)}, u32[]{:S(2)}) %all-to-all-start) | async-done | bytes 1048608 | tf_op jit(solution)/shard_map/all_to_all | solution.py:13
  28.7 1.7 multiply_add_fusion.5
  30.5 1.2 fusion.21
  34.1 77.8 %all-gather.13.cloned.1.call-done = f32[262144]{0:T(1024)} async-done(((f32[4096]{0:T(1024)}), f32[262144]{0:T(1024)}) %all-gather.13.cloned.1.call-update) | async-done | bytes 1048592 | tf_op jit(solution)/shard_map/all_gather | solution.py:20
  111.9 2.4 reshape.178
  114.3 59.7 %while.66 = (s32[]{:T(128)}, f32[4096]{0:T(1024)S(1)}, s32[]{:T(128)}, f32[64,4096]{1,0:T(8,128)}, s32[]{:T(128)}, /*index=5*/s32[]{:T(128)}, s32[]{:T(128)}, s32[]{:T(128)}) while((s32[]{:T(128)}, f32[4096]{0:T(1024)S(1)}, s32[]{:T(128)}, f32[64,4096]{1,0:T(8,128)}, s32[]{:T(128)}, /*index=5*/s32[]{:T(128)}, s32[]{:T(128)}, s32[]{:T(128)}) %tuple.128), condition=%wide.region_2.3_spmd, body=%wide.region_1.2_spmd.sunk | while | flops 4102 | bytes 82055 | solution.py:27
  176.7 1.9 fusion.20
  178.9 3.2 fusion.4
  182.0 65.4 %all-gather.15.cloned.1.call-done = f32[262144]{0:T(1024)} async-done(((f32[4096]{0:T(1024)}), f32[262144]{0:T(1024)}) %all-gather.15.cloned.1.call-update) | async-done | bytes 1048592 | tf_op jit(solution)/shard_map/all_gather | solution.py:20
  247.4 1.4 reshape.179
  248.9 2.0 fusion.23
  250.9 1.2 fusion.19
  252.2 77.3 %all-gather.17.cloned.1.call-done = f32[262144]{0:T(1024)} async-done(((f32[4096]{0:T(1024)}), f32[262144]{0:T(1024)}) %all-gather.17.cloned.1.call-update) | async-done | bytes 1048592 | tf_op jit(solution)/shard_map/all_gather | solution.py:20
  329.6 2.4 reshape.180
  331.9 59.7 %while.68 = (s32[]{:T(128)}, f32[4096]{0:T(1024)S(1)}, s32[]{:T(128)}, f32[64,4096]{1,0:T(8,128)}, s32[]{:T(128)}, /*index=5*/s32[]{:T(128)}, s32[]{:T(128)}, s32[]{:T(128)}) while((s32[]{:T(128)}, f32[4096]{0:T(1024)S(1)}, s32[]{:T(128)}, f32[64,4096]{1,0:T(8,128)}, s32[]{:T(128)}, /*index=5*/s32[]{:T(128)}, s32[]{:T(128)}, s32[]{:T(128)}) %tuple.134), condition=%wide.region_7.8_spmd, body=%wide.region_6.7_spmd.sunk | while | flops 4102 | bytes 82055 | solution.py:27
  393.7 1.9 fusion.18
  395.8 3.2 fusion.8
  399.0 66.1 %all-gather.19.cloned.1.call-done = f32[262144]{0:T(1024)} async-done(((f32[4096]{0:T(1024)}), f32[262144]{0:T(1024)}) %all-gather.19.cloned.1.call-update) | async-done | bytes 1048592 | tf_op jit(solution)/shard_map/all_gather | solution.py:20
  465.1 1.4 reshape.181
  466.6 2.0 fusion.22
  468.6 1.2 fusion.17
  469.9 77.3 %all-gather.21.cloned.1.call-done = f32[262144]{0:T(1024)} async-done(((f32[4096]{0:T(1024)}), f32[262144]{0:T(1024)}) %all-gather.21.cloned.1.call-update) | async-done | bytes 1048592 | tf_op jit(solution)/shard_map/all_gather | solution.py:20
  547.2 2.4 reshape.182
  549.6 59.7 %while.70 = (s32[]{:T(128)}, f32[4096]{0:T(1024)S(1)}, s32[]{:T(128)}, f32[64,4096]{1,0:T(8,128)}, s32[]{:T(128)}, /*index=5*/s32[]{:T(128)}, s32[]{:T(128)}, s32[]{:T(128)}) while((s32[]{:T(128)}, f32[4096]{0:T(1024)S(1)}, s32[]{:T(128)}, f32[64,4096]{1,0:T(8,128)}, s32[]{:T(128)}, /*index=5*/s32[]{:T(128)}, s32[]{:T(128)}, ...), condition=%wide.region_12.13_spmd, body=%wide.region_11.12_spmd.sunk | while | flops 4102 | bytes 82055 | solution.py:27
  609.3 1.2 multiply_subtract_fusion.4
  611.1 1.9 fusion.16
  613.3 1.8 fusion.12
  615.1 67.6 %all-gather.23.cloned.1.call-done = f32[262144]{0:T(1024)} async-done(((f32[4096]{0:T(1024)}), f32[262144]{0:T(1024)}) %all-gather.23.cloned.1.call-update) | async-done | bytes 1048592 | tf_op jit(solution)/shard_map/all_gather | solution.py:20
  682.7 1.4 reshape.183
  684.3 1.7 slice_subtract_fusion
  (449 shorter events, 182.4 us)
Async XLA Ops:
  7.2 21.5 %copy-start = (bf16[128,256]{1,0:T(8,128)(2,1)S(1)}, bf16[128,256]{1,0:T(8,128)(2,1)}, u32[]{:S(2)}) copy-start(bf16[128,256]{1,0:T(8,128)(2,1)} %param.19) | copy-start | bytes 196612
  7.2 7.0 %copy-start.7 = (f32[2,128]{1,0:T(2,128)S(1)}, f32[2,128]{1,0:T(2,128)}, u32[]{:S(2)}) copy-start(f32[2,128]{1,0:T(2,128)} %param.21) | copy-start | bytes 3076
  9.2 18.5 %all-to-all-start = ((bf16[4,512,256]{2,1,0:T(8,128)(2,1)}), bf16[4,512,256]{2,1,0:T(8,128)(2,1)S(1)}, u32[]{:S(2)}, u32[]{:S(2)}) async-start(bf16[4,512,256]{2,1,0:T(8,128)(2,1)} %stack.2), calls=%async_computation | async-start | bytes 2097152 | tf_op jit(solution)/shard_map/all_to_all | solution.py:13
  14.2 97.7 %all-gather.13.cloned.1.call-start = ((), (), s32[]{:S(2)}) async-start(), calls=%async_computation.1 | async-start | bytes 1064960 | tf_op jit(solution)/shard_map/all_gather | solution.py:20
  27.7 1.0 copy-start.1
  30.4 1.3 copy-start.6
  30.5 1.9 copy-start.5
  31.7 142.3 %copy-start.2 = (f32[4096]{0:T(1024)S(1)}, f32[4096]{0:T(1024)}, u32[]{:S(2)}) copy-start(f32[4096]{0:T(1024)} %fusion.21) | copy-start | bytes 49156
  31.7 215.7 %all-gather.15.cloned.1.call-start = ((), (), s32[]{:S(2)}) async-start(), calls=%async_computation.2 | async-start | bytes 1064960 | tf_op jit(solution)/shard_map/all_gather | solution.py:20
  32.6 143.3 %copy-start.8 = (f32[2,128]{1,0:T(2,128)S(1)}, f32[2,128]{1,0:T(2,128)}, u32[]{:S(2)}) copy-start(f32[2,128]{1,0:T(2,128)} %param.22) | copy-start | bytes 3076
  175.8 153.7 %all-gather.17.cloned.1.call-start = ((), (), s32[]{:S(2)}) async-start(), calls=%async_computation.3 | async-start | bytes 1064960 | tf_op jit(solution)/shard_map/all_gather | solution.py:20
  252.1 139.5 %copy-start.4 = (f32[4096]{0:T(1024)S(1)}, f32[4096]{0:T(1024)}, u32[]{:S(2)}) copy-start(f32[4096]{0:T(1024)} %fusion.19) | copy-start | bytes 49156
  252.2 212.9 %all-gather.19.cloned.1.call-start = ((), (), s32[]{:S(2)}) async-start(), calls=%async_computation.4 | async-start | bytes 1064960 | tf_op jit(solution)/shard_map/all_gather | solution.py:20
  393.5 153.7 %all-gather.21.cloned.1.call-start = ((), (), s32[]{:S(2)}) async-start(), calls=%async_computation.5 | async-start | bytes 1064960 | tf_op jit(solution)/shard_map/all_gather | solution.py:20
  469.8 139.5 %copy-start.3 = (f32[4096]{0:T(1024)S(1)}, f32[4096]{0:T(1024)}, u32[]{:S(2)}) copy-start(f32[4096]{0:T(1024)} %fusion.17) | copy-start | bytes 49156
  469.8 212.9 %all-gather.23.cloned.1.call-start = ((), (), s32[]{:S(2)}) async-start(), calls=%async_computation.6 | async-start | bytes 1064960 | tf_op jit(solution)/shard_map/all_gather | solution.py:20
Sparse Core Ops, SparseCore 0:
  31.8 80.0 all-gather.12
  175.9 71.4 all-gather.14
  252.3 77.2 all-gather.16
  393.6 71.4 all-gather.18
  469.9 77.2 all-gather.20
  611.3 71.4 all-gather.22
